TPU v7x, 512 devices: a whole 4x4x16 slice. The times are simulated.
512 devices in a mesh: grp: 16 (over y_hi, x, core), ops: 32 (over y_lo, z).
Axes of the slice: x: 4, y: 4 (y_hi: 2, y_lo: 2; y = y_hi * 2 + y_lo), z: 16, core: 2. Of those that a mesh axis runs over, the one named last changes fastest.
Arguments:
- psi: bfloat16 [112, 384, 384], P('grp', 'ops'), may hold values from -6 to 6
- left_ops: bfloat16 [112, 32, 384, 384], P('grp', 'ops'), may hold values from -1 to 2
- right_ops: bfloat16 [112, 32, 384, 384], P('grp', 'ops'), may hold values from -1 to 2
- right_group: int32 [112, 1], replicated, may hold values from 0 to 15; in each aligned block of 7 rows (0 to 6, 7 to 13, ...) no two rows name the same one
- right_slot: int32 [112], replicated, may hold values from 0 to 6
- precond_diag: float32 [112, 384, 384], P('grp', 'ops'), may hold values from 0.25 to 8
Outputs:
- sigma: float32 [112, 384, 384], P('grp', 'ops')
- correction: float32 [112, 384, 384], P('grp', 'ops')
Inputs may be any that keep to these rules, and one draw needn't show every extreme that they name: In the 7 sectors of one group, at most 1 have their right_group equal to any one group; some group reaches 1.
All inputs are finite; a program needn't handle non-finite values.
Results may differ from a plain program's by a relative error of at most 0.0006.
The roundings to bfloat16 on the way count: a program that leaves them out, or rounds other values in their place, can miss the bound.
Values may be sent and summed in bfloat16 or wider, within the bound.
No kernel may reach another device: no remote copies, remote signals or barrier semaphores. Data moves between devices by JAX's collectives and lax.ppermute only.
A program may use at most 64 MiB of HBM per device.

v0:
```python
import jax
import jax.numpy as jnp
from jax import lax
from jax.sharding import Mesh
from jax.sharding import PartitionSpec as P

GRP_OPS = ("grp_0", "grp_1", "grp_2", "ops_0", "ops_1")
GRP = ("grp_0", "grp_1", "grp_2")
OPS = ("ops_0", "ops_1")


def one_axis_at_a_time(array, axes):
    for axis in axes:
        array = lax.psum(array, axis)
    return array


def in_order(blocks, dim):
    blocks = jnp.moveaxis(blocks, 0, dim)
    lengths = blocks.shape
    return blocks.reshape(*lengths[:dim], lengths[dim] * lengths[dim + 1], *lengths[dim + 2 :])


def stacked_from(array, axes, order):
    blocks = array[None]
    for k in order:
        blocks = lax.all_gather(blocks, axes[k], axis=0, tiled=True)
    current = [lax.axis_size(axes[k]) for k in reversed(order)]
    blocks = blocks.reshape(*current, *array.shape)
    turned = sorted(range(len(order)), key=lambda place: order[len(order) - 1 - place])
    return blocks.transpose(*turned, *range(len(order), blocks.ndim)).reshape(-1, *array.shape)


def gather_axes(array, axes, order, dim):
    return in_order(stacked_from(array, axes, order), dim)


def sum_in_order(blocks, axes, order):
    lengths = [lax.axis_size(a) for a in axes]
    blocks = blocks.reshape(*lengths, *blocks.shape[1:])
    blocks = blocks.transpose(*order, *range(len(axes), blocks.ndim))
    blocks = blocks.reshape(-1, *blocks.shape[len(axes) :])
    for k in order:
        blocks = lax.psum_scatter(blocks, axes[k], scatter_dimension=0, tiled=True)
    return blocks[0]


def in_blocks(array, dim, length):
    lengths = array.shape
    blocks = array.reshape(*lengths[:dim], length, lengths[dim] // length, *lengths[dim + 1 :])
    return jnp.moveaxis(blocks, dim, 0)


def sum_by_axis(array, axes, order, dim):
    length = lax.axis_size(axes)
    return sum_in_order(in_blocks(array, dim, length), axes, order)


def early_sums(whole, partial_value, wave):
    whole_wave = whole.astype(jnp.float32)
    return (
        one_axis_at_a_time(jnp.sum(whole_wave * partial_value), GRP_OPS),
        one_axis_at_a_time(jnp.sum(wave * wave), GRP_OPS),
    )


def shards(psi, left_ops, right_ops, right_group, right_slot, precond_diag):
    groups = lax.axis_size(GRP)
    here = lax.axis_index(GRP)
    spg = psi.shape[0]
    cap = (spg + groups - 1) // groups
    owner = right_group[:, 0].reshape(groups, spg)
    slots = right_slot.reshape(groups, spg)
    match = owner == here
    rank = jnp.cumsum(match.astype(jnp.int32), axis=1) - 1
    places = jnp.arange(cap, dtype=jnp.int32)
    pick = match[:, None, :] & (rank[:, None, :] == places[None, :, None])
    source = jnp.sum(jnp.where(pick, slots[:, None, :], 0), axis=2).reshape(-1)
    mine = lax.dynamic_index_in_dim(owner, here, 0, keepdims=False)
    order_ids = jnp.arange(spg, dtype=jnp.int32)
    earlier = (mine[:, None] == mine[None, :]) & (order_ids[None, :] < order_ids[:, None])
    position = mine * cap + jnp.sum(earlier.astype(jnp.int32), axis=1)
    whole = gather_axes(psi, OPS, (0, 1), 1)
    outgoing = jnp.take(right_ops, source, axis=0)
    incoming = lax.all_to_all(outgoing, GRP, split_axis=0, concat_axis=0, tiled=True)
    partner_blocks = jnp.take(incoming, position, axis=0)
    images = jnp.einsum(
        "jac,jkdc->jkad", whole, partner_blocks, preferred_element_type=jnp.float32
    ).astype(jnp.bfloat16)
    wave = psi.astype(jnp.float32)
    partial_value = jnp.einsum(
        "jkab,jkbd->jad", left_ops, images, preferred_element_type=jnp.float32
    )
    correlation, norm_sq = early_sums(whole, partial_value, wave)
    sigma = sum_by_axis(partial_value, OPS, (1, 0), 1)
    theta = correlation / norm_sq
    gap = precond_diag - theta
    correction = (sigma - theta * wave) * gap / (gap * gap + 1.0)
    return (sigma, correction)


def solution(mesh):
    split = Mesh(
        mesh.devices.reshape(2, 4, 2, 2, 16), ("grp_0", "grp_1", "grp_2", "ops_0", "ops_1")
    )
    return jax.shard_map(
        shards,
        mesh=split,
        in_specs=(
            P(GRP, OPS, None),
            P(GRP, OPS, None, None),
            P(GRP, OPS, None, None),
            P(),
            P(),
            P(GRP, OPS, None),
        ),
        out_specs=(P(GRP, OPS, None), P(GRP, OPS, None)),
        check_vma=False,
    )
```

profile of v0, /device:TPU:8, one launch (start us, length us, event | category | flops | bytes accessed | tf_op | source)
XLA Modules:
  0.0 327.6 jit_solution(8427781241157373202)
XLA Ops:
  7.2 0.8 compare_reduce_fusion
  8.1 0.7 broadcast_in_dim_reshape.3
  9.2 3.4 %gather_fusion = bf16[16,384,384]{2,1,0:T(8,128)(2,1)} fusion(bf16[7,384,384]{2,1,0:T(8,128)(2,1)S(1)} %bitcast.56, s32[1024]{0:T(1024)S(1)} %pad_clamp_fusion.1), kind=kCustom, calls=%fused_computation | custom fusion | bytes 9437248 | tf_op jit(solution)/shard_map/jit(_take)/gather | solution.py:84
  12.6 5.1 %bitcast_select_fusion = bf16[16,1,384,384]{3,2,1,0:T(8,128)(2,1)} fusion(bf16[16,384,384]{2,1,0:T(8,128)(2,1)} %gather_fusion, pred[16]{0:T(512)(128)(4,1)S(1)} %compare_and_fusion), kind=kLoop, calls=%fused_computation.2 | loop fusion | flops 2359296 | bytes 9437200 | tf_op jit(solution)/shard_map/jit(_take)/select_n | solution.py:84
  17.7 6.3 %all-to-all-start = ((bf16[16,1,384,384]{3,2,1,0:T(8,128)(2,1)}), bf16[16,1,384,384]{3,2,1,0:T(8,128)(2,1)}, u32[]{:S(2)}, u32[]{:S(2)}) async-start(bf16[16,1,384,384]{3,2,1,0:T(8,128)(2,1)} %bitcast_select_fusion), calls=%async_computation | async-start | bytes 9437184 | tf_op jit(solution)/shard_map/all_to_all | solution.py:85
  24.1 52.0 %all-gather = bf16[14,12,384]{2,1,0:T(8,128)(2,1)S(1)} all-gather(bf16[7,12,384]{2,1,0:T(8,128)(2,1)S(1)} %copy.25), channel_id=2, replica_groups=mesh['grp_0'=2,'grp_1'=4,'grp_2'=2,'ops_0'=2,'ops_1'=16] {'ops_0'}, dimensions={0}, use_global_device_ids=true | all-gather | bytes 193536 | tf_op jit(solution)/shard_map/all_gather | solution.py:27
  76.1 0.7 copy.34
  76.9 0.5 broadcast.140
  77.4 0.7 reduce.8
  78.1 0.2 convert_reduce_fusion
  78.4 79.6 %all-gather.3.cloned.1.call-done = bf16[32,7,12,384]{3,1,0,2:T(8,128)(2,1)} async-done(((bf16[2,7,12,384]{3,1,0,2:T(8,128)(2,1)}), bf16[32,7,12,384]{3,1,0,2:T(8,128)(2,1)}) %all-gather.3.cloned.1.call-update) | async-done | bytes 2064400 | tf_op jit(solution)/shard_map/all_gather | solution.py:27
  158.0 3.3 %copy.27 = bf16[2,16,7,12,384]{4,2,3,1,0:T(8,128)(2,1)} copy(bf16[2,16,7,12,384]{4,2,0,1,3:T(8,128)(2,1)} %bitcast.59) | data formatting | bytes 4128768 | tf_op jit(solution)/shard_map/transpose | solution.py:31
  161.3 4.6 %gather_fusion.1 = bf16[7,384,384]{2,1,0:T(8,128)(2,1)} fusion(bf16[16,384,384]{2,1,0:T(8,128)(2,1)} %bitcast.5, s32[1024]{0:T(1024)S(1)} %pad_clamp_fusion), kind=kCustom, calls=%fused_computation.1 | custom fusion | bytes 4128796 | tf_op jit(solution)/shard_map/jit(_take)/gather | solution.py:86
  165.9 9.0 %multiply_reduce_fusion = (f32[]{:T(128)}, f32[7,384,384]{2,1,0:T(8,128)}) fusion(bf16[7,384,384]{2,0,1:T(8,128)(2,1)} %bitcast.60, bf16[7,1,384,384]{3,2,1,0:T(8,128)(2,1)} %param.7, bf16[7,384,384]{2,1,0:T(8,128)(2,1)} %gather_fusion.1, pred[7]{0:T(512)(128)(4,1)S(1)} %compare_and_fusion.1), kind=kOutput, calls=%fused_computation.3 | convolution fusion | flops 1590607872 | bytes 10321931 | tf_op jit(solution)/shard_map/jkab,jkbd->jad/dot_general | solution.py:91
  174.9 4.6 %copy.30 = f32[7,384,384]{2,0,1:T(8,128)S(1)} copy(f32[7,384,384]{2,1,0:T(8,128)} %get-tuple-element.13) | data formatting | bytes 8257536 | tf_op jit(solution)/shard_map/jkab,jkbd->jad/dot_general | solution.py:91
  179.5 2.5 copy.31
  182.1 79.2 %reduce-scatter.3.cloned.1.call-done = f32[2,7,12,384]{3,1,2,0:T(8,128)} async-done(((f32[32,7,12,384]{3,1,2,0:T(8,128)}), f32[2,7,12,384]{3,1,2,0:T(8,128)}) %reduce-scatter.3.cloned.1.call-update) | async-done | bytes 258064 | tf_op jit(solution)/shard_map/reduce_scatter | solution.py:44
  261.4 0.6 fusion.13
  262.0 7.0 %all-reduce.4 = (f32[]{:T(128)}, f32[]{:T(128)}) all-reduce(f32[]{:T(128)} %get-tuple-element.12, f32[]{:T(128)} %fusion.13), channel_id=1, replica_groups=mesh['grp_0'=2,'grp_1'=4,'grp_2'=2,'ops_0'=2,'ops_1'=16] {'grp_0'}, use_global_device_ids=true, to_apply=%region_6.7 | all-reduce | flops 2 | bytes 16 | tf_op jit(solution)/shard_map/psum | solution.py:14
  269.0 11.3 %all-reduce.1 = (f32[]{:T(128)}, f32[]{:T(128)}) all-reduce(f32[]{:T(128)} %get-tuple-element.10, f32[]{:T(128)} %get-tuple-element.11), channel_id=1, replica_groups=mesh['grp_0'=2,'grp_1'=4,'grp_2'=2,'ops_0'=2,'ops_1'=16] {'grp_1'}, use_global_device_ids=true, to_apply=%region_7.8 | all-reduce | flops 2 | bytes 16 | tf_op jit(solution)/shard_map/psum | solution.py:14
  280.3 3.1 all-reduce.3
  283.4 5.6 %all-reduce.2 = (f32[]{:T(128)}, f32[]{:T(128)}) all-reduce(f32[]{:T(128)} %get-tuple-element.8, f32[]{:T(128)} %get-tuple-element.9), channel_id=1, replica_groups=mesh['grp_0'=2,'grp_1'=4,'grp_2'=2,'ops_0'=2,'ops_1'=16] {'ops_0'}, use_global_device_ids=true, to_apply=%region_9.10 | all-reduce | flops 2 | bytes 16 | tf_op jit(solution)/shard_map/psum | solution.py:14
  289.0 29.2 %all-reduce = (f32[]{:T(128)}, f32[]{:T(128)}) all-reduce(f32[]{:T(128)} %get-tuple-element.6, f32[]{:T(128)} %get-tuple-element.7), channel_id=1, replica_groups=mesh['grp_0'=2,'grp_1'=4,'grp_2'=2,'ops_0'=2,'ops_1'=16] {'ops_1'}, use_global_device_ids=true, to_apply=%region_10.11 | all-reduce | flops 2 | bytes 16 | tf_op jit(solution)/shard_map/psum | solution.py:14
  319.5 1.6 fusion.16
  (29 shorter events, 0.8 us)
Async XLA Ops:
  7.2 2.0 copy-start
  17.7 6.4 %copy-start.1 = (bf16[7,12,384]{2,0,1:T(8,128)(2,1)S(1)}, bf16[7,12,384]{2,0,1:T(8,128)(2,1)}, u32[]{:S(2)}) copy-start(bf16[7,12,384]{2,0,1:T(8,128)(2,1)} %param.6) | copy-start | bytes 193540
  17.7 59.7 %copy-start.3 = (s32[112,1]{0,1:T(1,128)S(1)}, s32[112,1]{0,1:T(1,128)}, u32[]{:S(2)}) copy-start(s32[112,1]{0,1:T(1,128)} %param.9) | copy-start | bytes 1348
  17.7 143.6 %all-to-all-start = ((bf16[16,1,384,384]{3,2,1,0:T(8,128)(2,1)}), bf16[16,1,384,384]{3,2,1,0:T(8,128)(2,1)}, u32[]{:S(2)}, u32[]{:S(2)}) async-start(bf16[16,1,384,384]{3,2,1,0:T(8,128)(2,1)} %bitcast_select_fusion), calls=%async_computation | async-start | bytes 9437184 | tf_op jit(solution)/shard_map/all_to_all | solution.py:85
  24.0 134.0 %all-gather.3.cloned.1.call-start = ((), (), s32[]{:S(2)}) async-start(), calls=%async_computation.3 | async-start | bytes 2506752 | tf_op jit(solution)/shard_map/all_gather | solution.py:27
  76.8 184.5 %reduce-scatter.3.cloned.1.call-start = ((), (), s32[]{:S(2)}) async-start(), calls=%async_computation.4 | async-start | bytes 5013504 | tf_op jit(solution)/shard_map/reduce_scatter | solution.py:44
  182.0 137.4 %copy-start.2 = (f32[7,12,384]{2,0,1:T(8,128)S(1)}, f32[7,12,384]{2,0,1:T(8,128)}, u32[]{:S(2)}) copy-start(f32[7,12,384]{2,0,1:T(8,128)} %param.11) | copy-start | bytes 387076
  182.1 137.4 %reduce-scatter.5.cloned.1.call-start = ((), (), s32[]{:S(2)}) async-start(), calls=%async_computation.5 | async-start | bytes 442368 | tf_op jit(solution)/shard_map/reduce_scatter | solution.py:44
Sparse Core Ops, SparseCore 0:
  76.9 81.0 all-gather.2
  182.2 79.0 reduce-scatter.2
  264.7 19.3 reduce-scatter.4
where the time goes:
time: 328 us
  waiting for transfers between devices  159 us (48%)
  blocking collectives  108 us (33%)
  local copies, waits for them, and re-layouts  20.6 us (6%)
  between operations  15.1 us (5%)
  other arithmetic  9.36 us (3%)
  matrix products  9.01 us (3%)
  starting transfers between devices  6.44 us (2%)
    all_gather x1, waiting for transfers between devices, stacked_from(): blocks = lax.all_gather(blocks, axes[k], axis=0, tiled=True)  79.6 us
    reduce_scatter x2, waiting for transfers between devices, sum_in_order(): blocks = lax.psum_scatter(blocks, axes[k], scatter_dimension=0, tiled=True)  79.2 us
    psum x5, blocking collectives, one_axis_at_a_time(): array = lax.psum(array, axis)  56.2 us
    all_gather x1, blocking collectives, stacked_from(): blocks = lax.all_gather(blocks, axes[k], axis=0, tiled=True)  52 us
    dot_general x1, matrix products, shards(): jnp.einsum('jkab,jkbd->jad', left_ops, images, preferred_element_type=jnp...  9.01 us
  transfers between devices with their start and end apart: 4, of which 2 were waited for; matrix products, arithmetic and copies ran while one was open for 2% of the time, Pallas kernels for 0%

commit v1 on v0

v1 whole, which is shorter than its diff:
```python
import jax
import jax.numpy as jnp
from jax import lax
from jax.experimental import pallas as pl
from jax.experimental.pallas import tpu as pltpu
from jax.sharding import Mesh
from jax.sharding import PartitionSpec as P

GRP = ("yh", "x", "c")
OPS = ("yl", "z")
LANES = 128


def pick_kernel(groups_ref, slots_ref, me_ref, right_ref, out_ref):
    out_ref[...] = right_ref[...]


def outgoing_blocks(groups, slots, me, rights, n_groups):
    spg, rows, cols = rights.shape

    def source(g, groups_ref, slots_ref, me_ref):
        slot = 0
        for j in range(spg):
            named = groups_ref[g * spg + j] == me_ref[0]
            slot = jnp.where(named, slots_ref[g * spg + j], slot)
        return slot, 0, 0

    return pl.pallas_call(
        pick_kernel,
        grid_spec=pltpu.PrefetchScalarGridSpec(
            num_scalar_prefetch=3,
            grid=(n_groups,),
            in_specs=[pl.BlockSpec((1, rows, cols), source)],
            out_specs=pl.BlockSpec((1, rows, cols), lambda g, *_: (g, 0, 0)),
        ),
        out_shape=jax.ShapeDtypeStruct((n_groups, rows, cols), rights.dtype),
        name="pick",
    )(groups, slots, me, rights)


def sigma_kernel(shape, groups_ref, me_ref, half_ref, norm_ref, own_ref, other_ref, left_ref, right_ref, out_ref, psi_ref, part_ref, corr_ref):
    n_z, n_y, part, chunks, extra, stride = shape
    j = pl.program_id(0)
    spg = pl.num_programs(0)
    half = own_ref.shape[1]
    psi_ref[pl.ds(pl.multiple_of(half_ref[0] * half, half), half), :] = own_ref[0]
    psi_ref[pl.ds(pl.multiple_of((1 - half_ref[0]) * half, half), half), :] = other_ref[0]
    psi = psi_ref[...]
    image = lax.dot_general(psi, right_ref[0], (((1,), (1,)), ((), ())), preferred_element_type=jnp.float32)
    total = jnp.dot(left_ref[0], image.astype(jnp.bfloat16), preferred_element_type=jnp.float32)
    weighted = psi.astype(jnp.float32) * total
    folded = jnp.sum(weighted.reshape(-1, 8, weighted.shape[1]), axis=0)
    corr = sum(folded[:, c * LANES : (c + 1) * LANES] for c in range(chunks))

    @pl.when(j == 0)
    def _():
        corr_ref[...] = corr

    @pl.when(j > 0)
    def _():
        corr_ref[...] += corr

    for c in range(chunks):
        part_ref[c] = total[:, c * LANES : (c + 1) * LANES]
    width = chunks * part
    for y in range(n_y):
        for z in range(n_z):
            for c in range(chunks):
                rows = part_ref[c, pl.ds(y * half + z * part, part), :]
                out_ref[pl.ds(z * stride + y * spg_rows(shape) + c * part + j * width, part), :] = rows

    @pl.when(j == spg - 1)
    def _():
        top = jnp.sum(corr_ref[...], axis=0, keepdims=True)
        below = jnp.zeros((extra - 2, LANES), jnp.float32)
        tail = jnp.concatenate([top, norm_ref[...], below], axis=0)
        for z in range(n_z):
            out_ref[pl.ds((z + 1) * stride - extra, extra), :] = tail


def spg_rows(shape):
    n_z, n_y, part, chunks, extra, stride = shape
    return (stride - extra) // n_y


def partial_sums(groups, me, half, norm, own, other, lefts, incoming, shape):
    spg, rows, cols = lefts.shape
    n_z, n_y, part, chunks, extra, stride = shape

    def kernel(*refs):
        sigma_kernel(shape, *refs)

    sector = lambda j, *_: (j, 0, 0)
    return pl.pallas_call(
        kernel,
        grid_spec=pltpu.PrefetchScalarGridSpec(
            num_scalar_prefetch=3,
            grid=(spg,),
            in_specs=[
                pl.BlockSpec((1, LANES), lambda j, *_: (0, 0)),
                pl.BlockSpec((1, rows // n_y, cols), sector),
                pl.BlockSpec((1, rows // n_y, cols), sector),
                pl.BlockSpec((1, rows, cols), sector),
                pl.BlockSpec((1, rows, cols), lambda j, g, m, h: (g[m[0] * spg + j], 0, 0)),
            ],
            out_specs=pl.BlockSpec((n_z * stride, LANES), lambda j, *_: (0, 0)),
            scratch_shapes=[
                pltpu.VMEM((rows, cols), jnp.bfloat16),
                pltpu.VMEM((chunks, rows, LANES), jnp.float32),
                pltpu.VMEM((8, LANES), jnp.float32),
            ],
        ),
        out_shape=jax.ShapeDtypeStruct((n_z * stride, LANES), jnp.float32),
        name="partial",
    )(groups, me, half, norm, own, other, lefts, incoming)


def shards(psi, left_ops, right_ops, right_group, right_slot, precond_diag):
    n_groups, n_z, n_y = lax.axis_size(GRP), lax.axis_size("z"), lax.axis_size("yl")
    spg, part, cols = psi.shape
    chunks = cols // LANES
    me = lax.axis_index(GRP).astype(jnp.int32).reshape(1)
    half = lax.axis_index("yl").astype(jnp.int32)
    groups = right_group.reshape(-1)

    mine = jnp.transpose(psi, (1, 0, 2))
    theirs = lax.ppermute(mine, "yl", [(0, 1), (1, 0)])
    outgoing = outgoing_blocks(groups, right_slot, me, right_ops[:, 0], n_groups)
    incoming = lax.all_to_all(outgoing, GRP, split_axis=0, concat_axis=0, tiled=True)
    own = lax.all_gather(mine, "z", axis=0, tiled=True)
    other = lax.all_gather(theirs, "z", axis=0, tiled=True)
    own = jnp.transpose(own, (1, 0, 2))
    other = jnp.transpose(other, (1, 0, 2))

    wave = psi.astype(jnp.float32)
    norm = jnp.sum(jnp.sum(wave * wave, axis=(0, 1)).reshape(chunks, 1, LANES), axis=0)
    block = spg * part * chunks
    extra = 4
    stride = n_y * block + extra
    shape = (n_z, n_y, part, chunks, extra, stride)
    partials = partial_sums(groups, me, half.reshape(1), norm, own, other, left_ops[:, 0], incoming, shape)

    summed = lax.psum_scatter(partials, "z", scatter_dimension=0, tiled=True)
    summed = lax.optimization_barrier(summed)
    kept = lax.dynamic_slice_in_dim(summed, half * block, block, 0)
    given = lax.dynamic_slice_in_dim(summed, (1 - half) * block, block, 0)
    taken = lax.ppermute(given, "yl", [(0, 1), (1, 0)])
    scalars = summed[n_y * block : n_y * block + 2].reshape(1, 2, LANES)
    spread = ("yh", "x", "c", "yl")
    copies = jnp.broadcast_to(scalars, (lax.axis_size(spread), 2, LANES))
    both = jnp.sum(lax.all_to_all(copies, spread, split_axis=0, concat_axis=0, tiled=True), axis=(0, 2))
    theta = both[0] / both[1]
    sigma = (kept + taken).reshape(spg, chunks, part, LANES).transpose(0, 2, 1, 3).reshape(spg, part, cols)
    gap = precond_diag - theta
    correction = (sigma - theta * wave) * gap / (gap * gap + 1.0)
    return (sigma, correction)


def solution(mesh):
    split = Mesh(mesh.devices.reshape(2, 4, 2, 2, 16), GRP + OPS)
    return jax.shard_map(
        shards,
        mesh=split,
        in_specs=(
            P(GRP, OPS, None),
            P(GRP, OPS, None, None),
            P(GRP, OPS, None, None),
            P(),
            P(),
            P(GRP, OPS, None),
        ),
        out_specs=(P(GRP, OPS, None), P(GRP, OPS, None)),
        check_vma=False,
    )
```

time: 328 us -> 200 us (0.61)
  the two profiles are of different devices: /device:TPU:8 before, /device:TPU:1 now
where the time goes in v1:
time: 200 us; the launch traced here: 199 us
  blocking collectives  117 us (58%)
  starting transfers between devices  39.2 us (20%)
  Pallas kernels  22 us (11%)
  waiting for transfers between devices  11 us (6%)
  local copies, waits for them, and re-layouts  5.61 us (3%)
  between operations  2.8 us (1%)
    unnamed x1, blocking collectives  46.4 us
    all_gather x1, blocking collectives, shards(): own = lax.all_gather(mine, 'z', axis=0, tiled=True)  35.9 us
    all_gather x1, blocking collectives, shards(): other = lax.all_gather(theirs, 'z', axis=0, tiled=True)  34.7 us
    all_to_all x1, starting transfers between devices, shards(): lax.all_to_all(copies, spread, split_axis=0, concat_axis=0, tiled=True)  22 us
    pallas_call x1, Pallas kernels, outgoing_blocks(): pl.pallas_call(pick_kernel, grid_spec=pltpu.PrefetchScalarGridSpec(num_sc...  11.4 us
    pallas_call x1, Pallas kernels, partial_sums(): pl.pallas_call(kernel, grid_spec=pltpu.PrefetchScalarGridSpec(num_scalar_...  10.7 us
    all_to_all x1, starting transfers between devices, shards(): lax.all_to_all(outgoing, GRP, split_axis=0, concat_axis=0, tiled=True)  10.6 us
    ppermute x1, waiting for transfers between devices, shards(): theirs = lax.ppermute(mine, 'yl', [(0, 1), (1, 0)])  7.23 us
  transfers between devices with their start and end apart: 5, of which 2 were waited for; matrix products, arithmetic and copies ran while one was open for 2% of the time, Pallas kernels for 0%

profile of v1, /device:TPU:1, one launch (start us, length us, event | category | flops | bytes accessed | tf_op | source)
XLA Modules:
  0.0 199.1 jit_solution(3712429585739774909)
XLA Ops:
  0.6 11.4 %pick.1 = bf16[16,384,384]{2,1,0:T(8,128)(2,1)} custom-call(s32[112]{0:T(128)} %bitcast.29, s32[112]{0:T(128)} %slots_ref.1, s32[1]{0:T(128)} %bitcast.1.me_ref.refs_1_, bf16[7,384,384]{2,1,0:T(8,128)(2,1)} %bitcast.24), custom_call_target="tpu_custom_call" | custom-call | tf_op jit(solution)/shard_map/pick/pallas_call | solution.py:28
  12.0 10.6 %all-to-all-start = ((bf16[16,384,384]{2,1,0:T(8,128)(2,1)}), bf16[16,384,384]{2,1,0:T(8,128)(2,1)}, u32[]{:S(2)}, u32[]{:S(2)}) async-start(bf16[16,384,384]{2,1,0:T(8,128)(2,1)} %pick.1), calls=%async_computation | async-start | bytes 9437184 | tf_op jit(solution)/shard_map/all_to_all | solution.py:129
  22.6 1.9 collective-permute-start
  24.6 35.9 %all_gather.6 = bf16[192,7,384]{2,1,0:T(8,128)(2,1)S(1)} all-gather(bf16[12,7,384]{2,1,0:T(8,128)(2,1)S(1)} %bitcast.28), channel_id=1, replica_groups=mesh['yh'=2,'x'=4,'c'=2,'yl'=2,'z'=16] {'z'}, dimensions={0}, use_global_device_ids=true | all-gather | bytes 1096704 | tf_op jit(solution)/shard_map/all_gather | solution.py:130
  60.5 1.1 copy.28
  61.6 0.5 bitcast_reduce_fusion
  62.2 7.2 %collective-permute-done = bf16[12,7,384]{2,1,0:T(8,128)(2,1)S(1)} collective-permute-done((bf16[12,7,384]{2,1,0:T(8,128)(2,1)S(1)}, bf16[12,7,384]{2,1,0:T(8,128)(2,1)S(1)}, u32[]{:S(2)}, u32[]{:S(2)}) %collective-permute-start) | collective-permute-done | bytes 64544 | tf_op jit(solution)/shard_map/ppermute | solution.py:127
  69.4 34.7 %all_gather.7 = bf16[192,7,384]{2,1,0:T(8,128)(2,1)S(1)} all-gather(bf16[12,7,384]{2,1,0:T(8,128)(2,1)S(1)} %collective-permute-done), channel_id=1, replica_groups=mesh['yh'=2,'x'=4,'c'=2,'yl'=2,'z'=16] {'z'}, dimensions={0}, use_global_device_ids=true | all-gather | bytes 1096704 | tf_op jit(solution)/shard_map/all_gather | solution.py:131
  104.1 1.1 copy.27
  105.2 10.7 %partial.1 = f32[8128,128]{1,0:T(8,128)} custom-call(s32[112]{0:T(128)} %bitcast.30, s32[1]{0:T(128)} %bitcast.1.me_ref.refs_1_, s32[1]{0:T(128)} %bitcast.2.refs_2_, f32[1,128]{1,0:T(1,128)} %bitcast.31, bf16[7,192,384]{2,1,0:T(8,128)(2,1)} %bitcast.22, bf16[7,192,384]{2,1,0:T(8,128)(2,1)} %bitcast.23, bf16[7,384,384]{2,1,0:T(8,128)(2,1)} %bitcast.25, ...), custom_call_target="tpu_custom_call" | custom-call | tf_op jit(solution)/shard_map/partial/pallas_call | solution.py:94
  115.9 46.4 %fusion = f32[512,128]{1,0:T(8,128)S(1)} fusion(f32[8128,128]{1,0:T(8,128)} %partial.1), kind=kCustom, calls=%all-reduce-scatter | all-reduce-scatter fusion | flops 1048577 | bytes 4425728
  162.4 1.4 collective-permute-start.2
  163.8 1.3 dynamic-slice.4
  165.7 0.7 concatenate
  166.5 0.6 broadcast_in_dim.2
  167.1 22.0 %all-to-all-start.1 = ((f32[32,2,128]{2,1,0:T(2,128)}), f32[32,2,128]{2,1,0:T(2,128)S(1)}, u32[]{:S(2)}, u32[]{:S(2)}) async-start(f32[32,2,128]{2,1,0:T(2,128)} %broadcast_in_dim.2), calls=%async_computation.1 | async-start | bytes 65536 | tf_op jit(solution)/shard_map/all_to_all | solution.py:151
  189.1 3.3 %collective-permute-start.1 = (f32[252,128]{1,0:T(8,128)S(1)}, f32[252,128]{1,0:T(8,128)S(1)}, u32[]{:S(2)}, u32[]{:S(2)}) collective-permute-start(f32[252,128]{1,0:T(8,128)S(1)} %constant_dynamic-slice_fusion.1), channel_id=1, source_target_pairs={{0,16},{16,0},{1,17},{17,1},{2,18},{18,2},{3,19},{19,3},{4,20},{20... | collective-permute-start | bytes 387080 | tf_op jit(solution)/shard_map/ppermute | solution.py:147
  192.3 3.8 %all-to-all-done.1 = f32[32,2,128]{2,1,0:T(2,128)S(1)} async-done(((f32[32,2,128]{2,1,0:T(2,128)}), f32[32,2,128]{2,1,0:T(2,128)S(1)}, u32[]{:S(2)}, u32[]{:S(2)}) %all-to-all-start.1) | async-done | bytes 32800 | tf_op jit(solution)/shard_map/all_to_all | solution.py:151
  196.1 0.1 reduce_sum.32
  196.2 0.6 fusion.5
  198.2 0.1 copy.20
  198.3 0.1 reshape.31
  198.4 0.0 copy-start.1
  198.4 0.7 fusion.4
  (15 shorter events, 0.2 us)
Async XLA Ops:
  12.0 10.6 %copy-start = (bf16[7,12,384]{2,0,1:T(8,128)(2,1)S(1)}, bf16[7,12,384]{2,0,1:T(8,128)(2,1)}, u32[]{:S(2)}) copy-start(bf16[7,12,384]{2,0,1:T(8,128)(2,1)} %param.6) | copy-start | bytes 193540
  12.0 93.2 %all-to-all-start = ((bf16[16,384,384]{2,1,0:T(8,128)(2,1)}), bf16[16,384,384]{2,1,0:T(8,128)(2,1)}, u32[]{:S(2)}, u32[]{:S(2)}) async-start(bf16[16,384,384]{2,1,0:T(8,128)(2,1)} %pick.1), calls=%async_computation | async-start | bytes 9437184 | tf_op jit(solution)/shard_map/all_to_all | solution.py:129
  22.6 46.8 %collective-permute-start = (bf16[12,7,384]{2,1,0:T(8,128)(2,1)S(1)}, bf16[12,7,384]{2,1,0:T(8,128)(2,1)S(1)}, u32[]{:S(2)}, u32[]{:S(2)}) collective-permute-start(bf16[12,7,384]{2,1,0:T(8,128)(2,1)S(1)} %bitcast.27), channel_id=1, source_target_pairs={{0,16},{16,0},{1,17},{17,1},{2,18},{18,2},{3,19},{19,3},{4,20},{20... | collective-permute-start | bytes 193544 | tf_op jit(solution)/shard_map/ppermute | solution.py:127
  115.9 82.5 %copy-start.2 = (f32[7,12,384]{2,0,1:T(8,128)S(1)}, f32[7,12,384]{2,0,1:T(8,128)}, u32[]{:S(2)}) copy-start(f32[7,12,384]{2,0,1:T(8,128)} %param.11) | copy-start | bytes 387076
  162.4 3.4 %collective-permute-start.2 = (f32[60,128]{1,0:T(8,128)S(1)}, f32[60,128]{1,0:T(8,128)S(1)}, u32[]{:S(2)}, u32[]{:S(2)}) collective-permute-start(f32[60,128]{1,0:T(8,128)S(1)} %slice.13), channel_id=1, source_target_pairs={{0,1},{1,2},{2,3},{3,4},{4,5},{5,6},{6,7},{7,8},{8,9},{9,10},{10,1... | collective-permute-start | bytes 92168
  167.1 29.0 %all-to-all-start.1 = ((f32[32,2,128]{2,1,0:T(2,128)}), f32[32,2,128]{2,1,0:T(2,128)S(1)}, u32[]{:S(2)}, u32[]{:S(2)}) async-start(f32[32,2,128]{2,1,0:T(2,128)} %broadcast_in_dim.2), calls=%async_computation.1 | async-start | bytes 65536 | tf_op jit(solution)/shard_map/all_to_all | solution.py:151
  189.1 9.1 %collective-permute-start.1 = (f32[252,128]{1,0:T(8,128)S(1)}, f32[252,128]{1,0:T(8,128)S(1)}, u32[]{:S(2)}, u32[]{:S(2)}) collective-permute-start(f32[252,128]{1,0:T(8,128)S(1)} %constant_dynamic-slice_fusion.1), channel_id=1, source_target_pairs={{0,16},{16,0},{1,17},{17,1},{2,18},{18,2},{3,19},{19,3},{4,20},{20... | collective-permute-start | bytes 387080 | tf_op jit(solution)/shard_map/ppermute | solution.py:147
  198.4 0.7 copy-start.1

commit v2 on v1

--- a/solution.py
+++ b/solution.py
@@ -11,29 +11,39 @@
 LANES = 128
 
 
-def pick_kernel(groups_ref, slots_ref, me_ref, right_ref, out_ref):
-    out_ref[...] = right_ref[...]
+def pick_kernel(groups_ref, slots_ref, me_ref, right_ref, out_ref, held_ref, in_sems, out_sems):
+    spg, n_groups = held_ref.shape[0], out_ref.shape[0]
+    loads = [pltpu.make_async_copy(right_ref.at[j], held_ref.at[j], in_sems.at[j]) for j in range(spg)]
+    for load in loads:
+        load.start()
+    slots = []
+    for g in range(n_groups):
+        slot = jnp.int32(0)
+        for j in range(spg):
+            slot = jnp.where(groups_ref[g * spg + j] == me_ref[0], slots_ref[g * spg + j], slot)
+        slots.append(slot)
+    for load in loads:
+        load.wait()
+    stores = [pltpu.make_async_copy(held_ref.at[slots[g]], out_ref.at[g], out_sems.at[g]) for g in range(n_groups)]
+    for store in stores:
+        store.start()
+    for store in stores:
+        store.wait()
 
 
 def outgoing_blocks(groups, slots, me, rights, n_groups):
     spg, rows, cols = rights.shape
-
-    def source(g, groups_ref, slots_ref, me_ref):
-        slot = 0
-        for j in range(spg):
-            named = groups_ref[g * spg + j] == me_ref[0]
-            slot = jnp.where(named, slots_ref[g * spg + j], slot)
-        return slot, 0, 0
-
+    scalars = pl.BlockSpec(memory_space=pltpu.SMEM)
     return pl.pallas_call(
         pick_kernel,
-        grid_spec=pltpu.PrefetchScalarGridSpec(
-            num_scalar_prefetch=3,
-            grid=(n_groups,),
-            in_specs=[pl.BlockSpec((1, rows, cols), source)],
-            out_specs=pl.BlockSpec((1, rows, cols), lambda g, *_: (g, 0, 0)),
-        ),
+        in_specs=[scalars, scalars, scalars, pl.BlockSpec(memory_space=pl.ANY)],
+        out_specs=pl.BlockSpec(memory_space=pl.ANY),
         out_shape=jax.ShapeDtypeStruct((n_groups, rows, cols), rights.dtype),
+        scratch_shapes=[
+            pltpu.VMEM((spg, rows, cols), rights.dtype),
+            pltpu.SemaphoreType.DMA((spg,)),
+            pltpu.SemaphoreType.DMA((n_groups,)),
+        ],
         name="pick",
     )(groups, slots, me, rights)
 
@@ -79,13 +89,13 @@
 
 
 def spg_rows(shape):
-    n_z, n_y, part, chunks, extra, stride = shape
+    _, n_y, _, _, extra, stride = shape
     return (stride - extra) // n_y
 
 
 def partial_sums(groups, me, half, norm, own, other, lefts, incoming, shape):
     spg, rows, cols = lefts.shape
-    n_z, n_y, part, chunks, extra, stride = shape
+    n_z, n_y, _, chunks, _, stride = shape
 
     def kernel(*refs):
         sigma_kernel(shape, *refs)
@@ -115,7 +125,7 @@
     )(groups, me, half, norm, own, other, lefts, incoming)
 
 
-def shards(psi, left_ops, right_ops, right_group, right_slot, precond_diag):
+def step(psi, left_ops, right_ops, right_group, right_slot, precond_diag):
     n_groups, n_z, n_y = lax.axis_size(GRP), lax.axis_size("z"), lax.axis_size("yl")
     spg, part, cols = psi.shape
     chunks = cols // LANES
@@ -124,13 +134,11 @@
     groups = right_group.reshape(-1)
 
     mine = jnp.transpose(psi, (1, 0, 2))
-    theirs = lax.ppermute(mine, "yl", [(0, 1), (1, 0)])
     outgoing = outgoing_blocks(groups, right_slot, me, right_ops[:, 0], n_groups)
     incoming = lax.all_to_all(outgoing, GRP, split_axis=0, concat_axis=0, tiled=True)
     own = lax.all_gather(mine, "z", axis=0, tiled=True)
-    other = lax.all_gather(theirs, "z", axis=0, tiled=True)
     own = jnp.transpose(own, (1, 0, 2))
-    other = jnp.transpose(other, (1, 0, 2))
+    other = lax.ppermute(own, "yl", [(0, 1), (1, 0)])
 
     wave = psi.astype(jnp.float32)
     norm = jnp.sum(jnp.sum(wave * wave, axis=(0, 1)).reshape(chunks, 1, LANES), axis=0)
@@ -148,7 +156,8 @@
     scalars = summed[n_y * block : n_y * block + 2].reshape(1, 2, LANES)
     spread = ("yh", "x", "c", "yl")
     copies = jnp.broadcast_to(scalars, (lax.axis_size(spread), 2, LANES))
-    both = jnp.sum(lax.all_to_all(copies, spread, split_axis=0, concat_axis=0, tiled=True), axis=(0, 2))
+    copies = lax.all_to_all(copies, spread, split_axis=0, concat_axis=0, tiled=True)
+    both = jnp.sum(copies, axis=(0, 2))
     theta = both[0] / both[1]
     sigma = (kept + taken).reshape(spg, chunks, part, LANES).transpose(0, 2, 1, 3).reshape(spg, part, cols)
     gap = precond_diag - theta
@@ -159,7 +168,7 @@
 def solution(mesh):
     split = Mesh(mesh.devices.reshape(2, 4, 2, 2, 16), GRP + OPS)
     return jax.shard_map(
-        shards,
+        step,
         mesh=split,
         in_specs=(
             P(GRP, OPS, None),

time: 200 us -> 183 us (0.915)
  waiting for transfers between devices: 11 us -> 38.5 us
  blocking collectives: 117 us -> 91.9 us
  starting transfers between devices: 39.2 us -> 28 us
  Pallas kernels: 22 us -> 15.2 us
    all_gather x2 -> x1, blocking collectives: 70.6 us -> 35.3 us  [step(): own = lax.all_gather(mine, 'z', axis=0, tiled=True)]
    ppermute x2, waiting for transfers between devices: 7.23 us -> 34.7 us  [the longest x1 34.7 us: step(): other = lax.ppermute(own, 'yl', [(0, 1), (1, 0)])]
    all_to_all x2, starting transfers between devices: 32.6 us -> 20.2 us  [the longest x1 11.3 us: step(): lax.all_to_all(outgoing, GRP, split_axis=0, concat_axis=0, tiled=True)]
    unnamed x1, blocking collectives: 46.4 us -> 56.6 us
    pallas_call x1, Pallas kernels: 11.4 us -> 4.53 us  [outgoing_blocks(): pl.pallas_call(pick_kernel, in_specs=[scalars, scalars, scalars, pl.Block...]
    all_gather x2 -> x1, local copies, waits for them, and re-layouts: 2.22 us -> 0.13 us  [step(): own = lax.all_gather(mine, 'z', axis=0, tiled=True)]
where the time goes in v2:
time: 183 us; the launch traced here: 182 us
  blocking collectives  91.9 us (50%)
  waiting for transfers between devices  38.5 us (21%)
  starting transfers between devices  28 us (15%)
  Pallas kernels  15.2 us (8%)
  local copies, waits for them, and re-layouts  4.5 us (2%)
  between operations  2.82 us (2%)
    unnamed x1, blocking collectives  56.6 us
    all_gather x1, blocking collectives, step(): own = lax.all_gather(mine, 'z', axis=0, tiled=True)  35.3 us
    ppermute x1, waiting for transfers between devices, step(): other = lax.ppermute(own, 'yl', [(0, 1), (1, 0)])  34.7 us
    all_to_all x1, starting transfers between devices, step(): lax.all_to_all(outgoing, GRP, split_axis=0, concat_axis=0, tiled=True)  11.3 us
    pallas_call x1, Pallas kernels, partial_sums(): pl.pallas_call(kernel, grid_spec=pltpu.PrefetchScalarGridSpec(num_scalar_...  10.7 us
    all_to_all x1, starting transfers between devices, step(): lax.all_to_all(copies, spread, split_axis=0, concat_axis=0, tiled=True)  8.98 us
    pallas_call x1, Pallas kernels, outgoing_blocks(): pl.pallas_call(pick_kernel, in_specs=[scalars, scalars, scalars, pl.Block...  4.53 us
    all_to_all x1, waiting for transfers between devices, step(): lax.all_to_all(copies, spread, split_axis=0, concat_axis=0, tiled=True)  3.75 us
  transfers between devices with their start and end apart: 5, of which 2 were waited for; matrix products, arithmetic and copies ran while one was open for 2% of the time, Pallas kernels for 0%

profile of v2, /device:TPU:1, one launch (start us, length us, event | category | flops | bytes accessed | tf_op | source)
XLA Modules:
  0.0 182.4 jit_solution(5459522503763172097)
XLA Ops:
  0.6 4.5 %pick.1 = bf16[16,384,384]{2,1,0:T(8,128)(2,1)} custom-call(s32[112]{0:T(128)} %bitcast.25, s32[112]{0:T(128)} %slots_ref.1, s32[1]{0:T(128)} %bitcast.1.me_ref.refs_1_, bf16[7,384,384]{2,1,0:T(8,128)(2,1)} %bitcast.21), custom_call_target="tpu_custom_call" | custom-call | tf_op jit(solution)/shard_map/pick/pallas_call | solution.py:37
  5.2 0.0 copy-start.2
  5.2 11.3 %all-to-all-start = ((bf16[16,384,384]{2,1,0:T(8,128)(2,1)}), bf16[16,384,384]{2,1,0:T(8,128)(2,1)}, u32[]{:S(2)}, u32[]{:S(2)}) async-start(bf16[16,384,384]{2,1,0:T(8,128)(2,1)} %pick.1), calls=%async_computation | async-start | bytes 9437184 | tf_op jit(solution)/shard_map/all_to_all | solution.py:138
  16.5 35.3 %all_gather.3 = bf16[192,7,384]{2,1,0:T(8,128)(2,1)S(1)} all-gather(bf16[12,7,384]{2,1,0:T(8,128)(2,1)S(1)} %bitcast.24), channel_id=1, replica_groups=mesh['yh'=2,'x'=4,'c'=2,'yl'=2,'z'=16] {'z'}, dimensions={0}, use_global_device_ids=true | all-gather | bytes 1096704 | tf_op jit(solution)/shard_map/all_gather | solution.py:139
  51.8 0.1 copy.23
  51.9 2.3 %collective-permute-start = (bf16[7,192,384]{2,1,0:T(8,128)(2,1)S(1)}, bf16[7,192,384]{2,1,0:T(8,128)(2,1)S(1)}, u32[]{:S(2)}, u32[]{:S(2)}) collective-permute-start(bf16[7,192,384]{2,1,0:T(8,128)(2,1)S(1)} %bitcast.19), channel_id=1, source_target_pairs={{0,16},{16,0},{1,17},{17,1},{2,18},{18,2},{3,19},{19,3},{4,20},{20... | collective-permute-start | bytes 3096584 | tf_op jit(solution)/shard_map/ppermute | solution.py:141
  54.3 0.6 bitcast_reduce_fusion
  54.8 34.7 %collective-permute-done.refs_5_ = bf16[7,192,384]{2,1,0:T(8,128)(2,1)S(1)} collective-permute-done((bf16[7,192,384]{2,1,0:T(8,128)(2,1)S(1)}, bf16[7,192,384]{2,1,0:T(8,128)(2,1)S(1)}, u32[]{:S(2)}, u32[]{:S(2)}) %collective-permute-start) | collective-permute-done | bytes 1032224 | tf_op jit(solution)/shard_map/ppermute | solution.py:141
  89.5 1.0 copy-done.1
  90.5 10.7 %partial.1 = f32[8128,128]{1,0:T(8,128)} custom-call(s32[112]{0:T(128)} %bitcast.26, s32[1]{0:T(128)} %bitcast.1.me_ref.refs_1_, s32[1]{0:T(128)} %bitcast.2.refs_2_, f32[1,128]{1,0:T(1,128)} %bitcast.27, bf16[7,192,384]{2,1,0:T(8,128)(2,1)} %bitcast.20, bf16[7,192,384]{2,1,0:T(8,128)(2,1)} %copy-done.1, bf16[7,384,384]{2,1,0:T(8,128)(2,1)} %bitcast.22, ...), custom_call_target="tpu_custom_call" | custom-call | tf_op jit(solution)/shard_map/partial/pallas_call | solution.py:104
  101.2 56.6 %fusion = f32[512,128]{1,0:T(8,128)S(1)} fusion(f32[8128,128]{1,0:T(8,128)} %partial.1), kind=kCustom, calls=%all-reduce-scatter | all-reduce-scatter fusion | flops 1048577 | bytes 4425728
  157.8 2.2 %collective-permute-start.2 = (f32[60,128]{1,0:T(8,128)S(1)}, f32[60,128]{1,0:T(8,128)S(1)}, u32[]{:S(2)}, u32[]{:S(2)}) collective-permute-start(f32[60,128]{1,0:T(8,128)S(1)} %slice.13), channel_id=1, source_target_pairs={{0,1},{1,2},{2,3},{3,4},{4,5},{5,6},{6,7},{7,8},{8,9},{9,10},{10,1... | collective-permute-start | bytes 92168
  160.0 1.3 dynamic-slice.4
  162.0 0.7 concatenate
  162.7 0.6 broadcast_in_dim.2
  163.3 9.0 %all-to-all-start.1 = ((f32[32,2,128]{2,1,0:T(2,128)}), f32[32,2,128]{2,1,0:T(2,128)S(1)}, u32[]{:S(2)}, u32[]{:S(2)}) async-start(f32[32,2,128]{2,1,0:T(2,128)} %broadcast_in_dim.2), calls=%async_computation.1 | async-start | bytes 65536 | tf_op jit(solution)/shard_map/all_to_all | solution.py:159
  172.4 3.3 %collective-permute-start.1 = (f32[252,128]{1,0:T(8,128)S(1)}, f32[252,128]{1,0:T(8,128)S(1)}, u32[]{:S(2)}, u32[]{:S(2)}) collective-permute-start(f32[252,128]{1,0:T(8,128)S(1)} %constant_dynamic-slice_fusion.1), channel_id=1, source_target_pairs={{0,16},{16,0},{1,17},{17,1},{2,18},{18,2},{3,19},{19,3},{4,20},{20... | collective-permute-start | bytes 387080 | tf_op jit(solution)/shard_map/ppermute | solution.py:155
  175.6 3.8 %all-to-all-done.1 = f32[32,2,128]{2,1,0:T(2,128)S(1)} async-done(((f32[32,2,128]{2,1,0:T(2,128)}), f32[32,2,128]{2,1,0:T(2,128)S(1)}, u32[]{:S(2)}, u32[]{:S(2)}) %all-to-all-start.1) | async-done | bytes 32800 | tf_op jit(solution)/shard_map/all_to_all | solution.py:159
  179.4 0.1 reduce_sum.32
  179.5 0.6 fusion.5
  181.5 0.1 copy.17
  181.6 0.1 reshape.31
  181.7 0.0 copy-start.3
  181.7 0.7 fusion.4
  (17 shorter events, 0.2 us)
Async XLA Ops:
  5.2 11.3 %copy-start.2 = (bf16[7,12,384]{2,0,1:T(8,128)(2,1)S(1)}, bf16[7,12,384]{2,0,1:T(8,128)(2,1)}, u32[]{:S(2)}) copy-start(bf16[7,12,384]{2,0,1:T(8,128)(2,1)} %param.6) | copy-start | bytes 193540
  5.2 84.3 %all-to-all-start = ((bf16[16,384,384]{2,1,0:T(8,128)(2,1)}), bf16[16,384,384]{2,1,0:T(8,128)(2,1)}, u32[]{:S(2)}, u32[]{:S(2)}) async-start(bf16[16,384,384]{2,1,0:T(8,128)(2,1)} %pick.1), calls=%async_computation | async-start | bytes 9437184 | tf_op jit(solution)/shard_map/all_to_all | solution.py:138
  51.9 37.6 %copy-start = (bf16[192,7,384]{2,0,1:T(8,128)(2,1)}, bf16[192,7,384]{2,0,1:T(8,128)(2,1)S(1)}, u32[]{:S(2)}) copy-start(bf16[192,7,384]{2,0,1:T(8,128)(2,1)S(1)} %copy.23) | copy-start | bytes 3096580
  51.9 37.6 %collective-permute-start = (bf16[7,192,384]{2,1,0:T(8,128)(2,1)S(1)}, bf16[7,192,384]{2,1,0:T(8,128)(2,1)S(1)}, u32[]{:S(2)}, u32[]{:S(2)}) collective-permute-start(bf16[7,192,384]{2,1,0:T(8,128)(2,1)S(1)} %bitcast.19), channel_id=1, source_target_pairs={{0,16},{16,0},{1,17},{17,1},{2,18},{18,2},{3,19},{19,3},{4,20},{20... | collective-permute-start | bytes 3096584 | tf_op jit(solution)/shard_map/ppermute | solution.py:141
  89.5 1.0 copy-start.1
  101.2 80.5 %copy-start.4 = (f32[7,12,384]{2,0,1:T(8,128)S(1)}, f32[7,12,384]{2,0,1:T(8,128)}, u32[]{:S(2)}) copy-start(f32[7,12,384]{2,0,1:T(8,128)} %param.11) | copy-start | bytes 387076
  157.8 4.1 %collective-permute-start.2 = (f32[60,128]{1,0:T(8,128)S(1)}, f32[60,128]{1,0:T(8,128)S(1)}, u32[]{:S(2)}, u32[]{:S(2)}) collective-permute-start(f32[60,128]{1,0:T(8,128)S(1)} %slice.13), channel_id=1, source_target_pairs={{0,1},{1,2},{2,3},{3,4},{4,5},{5,6},{6,7},{7,8},{8,9},{9,10},{10,1... | collective-permute-start | bytes 92168
  163.3 16.0 %all-to-all-start.1 = ((f32[32,2,128]{2,1,0:T(2,128)}), f32[32,2,128]{2,1,0:T(2,128)S(1)}, u32[]{:S(2)}, u32[]{:S(2)}) async-start(f32[32,2,128]{2,1,0:T(2,128)} %broadcast_in_dim.2), calls=%async_computation.1 | async-start | bytes 65536 | tf_op jit(solution)/shard_map/all_to_all | solution.py:159
  172.4 9.1 %collective-permute-start.1 = (f32[252,128]{1,0:T(8,128)S(1)}, f32[252,128]{1,0:T(8,128)S(1)}, u32[]{:S(2)}, u32[]{:S(2)}) collective-permute-start(f32[252,128]{1,0:T(8,128)S(1)} %constant_dynamic-slice_fusion.1), channel_id=1, source_target_pairs={{0,16},{16,0},{1,17},{17,1},{2,18},{18,2},{3,19},{19,3},{4,20},{20... | collective-permute-start | bytes 387080 | tf_op jit(solution)/shard_map/ppermute | solution.py:155
  181.7 0.7 copy-start.3

commit v3 on v2

v3 whole, which is shorter than its diff:
```python
import jax
import jax.numpy as jnp
from jax import lax
from jax.experimental import pallas as pl
from jax.experimental.pallas import tpu as pltpu
from jax.sharding import Mesh
from jax.sharding import PartitionSpec as P

GRP = ("yh", "x", "c")
COLUMN = ("zh", "zl")
OPS = ("yl",) + COLUMN
LANES = 128


def pick_kernel(groups_ref, slots_ref, me_ref, right_ref, out_ref, held_ref, in_sems, out_sems):
    spg, n_groups = held_ref.shape[0], out_ref.shape[0]
    loads = [pltpu.make_async_copy(right_ref.at[j], held_ref.at[j], in_sems.at[j]) for j in range(spg)]
    for load in loads:
        load.start()
    slots = []
    for g in range(n_groups):
        slot = jnp.int32(0)
        for j in range(spg):
            slot = jnp.where(groups_ref[g * spg + j] == me_ref[0], slots_ref[g * spg + j], slot)
        slots.append(slot)
    for load in loads:
        load.wait()
    stores = [pltpu.make_async_copy(held_ref.at[slots[g]], out_ref.at[g], out_sems.at[g]) for g in range(n_groups)]
    for store in stores:
        store.start()
    for store in stores:
        store.wait()


def outgoing_blocks(groups, slots, me, rights, n_groups):
    spg, rows, cols = rights.shape
    scalars = pl.BlockSpec(memory_space=pltpu.SMEM)
    return pl.pallas_call(
        pick_kernel,
        in_specs=[scalars, scalars, scalars, pl.BlockSpec(memory_space=pl.ANY)],
        out_specs=pl.BlockSpec(memory_space=pl.ANY),
        out_shape=jax.ShapeDtypeStruct((n_groups, rows, cols), rights.dtype),
        scratch_shapes=[
            pltpu.VMEM((spg, rows, cols), rights.dtype),
            pltpu.SemaphoreType.DMA((spg,)),
            pltpu.SemaphoreType.DMA((n_groups,)),
        ],
        name="pick",
    )(groups, slots, me, rights)


def sigma_kernel(shape, groups_ref, me_ref, place_ref, norm_ref, own_ref, other_ref, left_ref, right_ref, out_ref, stage_ref, rows_ref, psi_ref, image_ref, part_ref, corr_ref):
    n_z, n_y, part, chunks, extra, stride, spg = shape
    step_id = pl.program_id(0)
    half = n_z * part
    now, before = lax.rem(step_id, 2), lax.rem(step_id + 1, 2)
    sector = jnp.maximum(step_id - 1, 0)

    total = jnp.dot(left_ref[0], image_ref[before], preferred_element_type=jnp.float32)

    for source, held_ref in enumerate((own_ref, other_ref)):
        low = place_ref[1] if source == 0 else 1 - place_ref[1]
        for c in range(chunks):
            stage_ref[source, c] = held_ref[0, :, c * LANES : (c + 1) * LANES].astype(jnp.float32)
        for high in range(n_z // 2):
            for side in range(n_y):
                y = place_ref[0] if side == 0 else 1 - place_ref[0]
                start = y * half + (2 * high + low) * part
                for c in range(chunks):
                    rows_ref[c, pl.ds(start, part), :] = stage_ref[source, c, pl.ds((high * n_y + side) * part, part), :]
    for c in range(chunks):
        psi_ref[now, :, c * LANES : (c + 1) * LANES] = rows_ref[c].astype(jnp.bfloat16)
    image = lax.dot_general(psi_ref[now], right_ref[0], (((1,), (1,)), ((), ())), preferred_element_type=jnp.float32)
    image_ref[now] = image.astype(jnp.bfloat16)

    weighted = psi_ref[before].astype(jnp.float32) * total
    folded = jnp.sum(weighted.reshape(-1, 8, weighted.shape[1]), axis=0)
    corr = sum(folded[:, c * LANES : (c + 1) * LANES] for c in range(chunks))
    first = step_id == 1
    corr_ref[...] = jnp.where(first, corr, corr_ref[...] + corr)

    for c in range(chunks):
        part_ref[c] = total[:, c * LANES : (c + 1) * LANES]
    width = chunks * part
    block = spg * width
    for y in range(n_y):
        for z in range(n_z):
            for c in range(chunks):
                rows = part_ref[c, pl.ds(y * half + z * part, part), :]
                out_ref[pl.ds(z * stride + y * block + c * part + sector * width, part), :] = rows

    @pl.when(step_id == spg)
    def _():
        top = jnp.sum(corr_ref[...], axis=0, keepdims=True)
        below = jnp.zeros((extra - 2, LANES), jnp.float32)
        tail = jnp.concatenate([top, norm_ref[...], below], axis=0)
        for z in range(n_z):
            out_ref[pl.ds((z + 1) * stride - extra, extra), :] = tail


def partial_sums(groups, me, place, norm, own, other, lefts, incoming, shape):
    spg, rows, cols = lefts.shape
    n_z, _, _, chunks, _, stride = shape

    def kernel(*refs):
        sigma_kernel(shape + (spg,), *refs)

    def owner(j, groups_ref, me_ref, place_ref):
        return groups_ref[me_ref[0] * spg + jnp.minimum(j, spg - 1)], 0, 0

    half_rows = pl.BlockSpec((1, rows // 2, cols), lambda j, *_: (jnp.minimum(j, spg - 1), 0, 0))
    return pl.pallas_call(
        kernel,
        grid_spec=pltpu.PrefetchScalarGridSpec(
            num_scalar_prefetch=3,
            grid=(spg + 1,),
            in_specs=[
                pl.BlockSpec((1, LANES), lambda j, *_: (0, 0)),
                half_rows,
                half_rows,
                pl.BlockSpec((1, rows, cols), lambda j, *_: (jnp.maximum(j - 1, 0), 0, 0)),
                pl.BlockSpec((1, rows, cols), owner),
            ],
            out_specs=pl.BlockSpec((n_z * stride, LANES), lambda j, *_: (0, 0)),
            scratch_shapes=[
                pltpu.VMEM((2, chunks, rows // 2, LANES), jnp.float32),
                pltpu.VMEM((chunks, rows, LANES), jnp.float32),
                pltpu.VMEM((2, rows, cols), jnp.bfloat16),
                pltpu.VMEM((2, rows, cols), jnp.bfloat16),
                pltpu.VMEM((chunks, rows, LANES), jnp.float32),
                pltpu.VMEM((8, LANES), jnp.float32),
            ],
        ),
        out_shape=jax.ShapeDtypeStruct((n_z * stride, LANES), jnp.float32),
        name="partial",
    )(groups, me, place, norm, own, other, lefts, incoming)


def step(psi, left_ops, right_ops, right_group, right_slot, precond_diag):
    n_groups, n_z, n_y = lax.axis_size(GRP), lax.axis_size(COLUMN), lax.axis_size("yl")
    spg, part, cols = psi.shape
    chunks = cols // LANES
    me = lax.axis_index(GRP).astype(jnp.int32).reshape(1)
    half = lax.axis_index("yl").astype(jnp.int32)
    groups = right_group.reshape(-1)

    swap = [(0, 1), (1, 0)]
    mine = jnp.transpose(psi, (1, 0, 2))
    theirs = lax.ppermute(mine, "yl", swap)
    outgoing = outgoing_blocks(groups, right_slot, me, right_ops[:, 0], n_groups)
    incoming = lax.all_to_all(outgoing, GRP, split_axis=0, concat_axis=0, tiled=True)
    own = lax.all_gather(jnp.concatenate([mine, theirs], axis=0), "zh", axis=0, tiled=True)
    own = jnp.transpose(own, (1, 0, 2))
    other = lax.ppermute(own, "zl", swap)

    wave = psi.astype(jnp.float32)
    norm = jnp.sum(jnp.sum(wave * wave, axis=(0, 1)).reshape(chunks, 1, LANES), axis=0)
    block = spg * part * chunks
    extra = 4
    stride = n_y * block + extra
    shape = (n_z, n_y, part, chunks, extra, stride)
    place = jnp.stack([half, lax.axis_index("zl").astype(jnp.int32)])
    partials = partial_sums(groups, me, place, norm, own, other, left_ops[:, 0], incoming, shape)

    summed = lax.psum_scatter(partials, COLUMN, scatter_dimension=0, tiled=True)
    summed = lax.optimization_barrier(summed)
    kept = lax.dynamic_slice_in_dim(summed, half * block, block, 0)
    given = lax.dynamic_slice_in_dim(summed, (1 - half) * block, block, 0)
    taken = lax.ppermute(given, "yl", swap)
    scalars = summed[n_y * block : n_y * block + 2].reshape(1, 2, LANES)
    spread = ("yh", "x", "c", "yl")
    copies = jnp.broadcast_to(scalars, (lax.axis_size(spread), 2, LANES))
    copies = lax.all_to_all(copies, spread, split_axis=0, concat_axis=0, tiled=True)
    both = jnp.sum(copies, axis=(0, 2))
    theta = both[0] / both[1]
    sigma = (kept + taken).reshape(spg, chunks, part, LANES).transpose(0, 2, 1, 3).reshape(spg, part, cols)
    gap = precond_diag - theta
    correction = (sigma - theta * wave) * gap / (gap * gap + 1.0)
    return (sigma, correction)


def solution(mesh):
    split = Mesh(mesh.devices.reshape(2, 4, 2, 2, 8, 2), GRP + OPS)
    return jax.shard_map(
        step,
        mesh=split,
        in_specs=(
            P(GRP, OPS, None),
            P(GRP, OPS, None, None),
            P(GRP, OPS, None, None),
            P(),
            P(),
            P(GRP, OPS, None),
        ),
        out_specs=(P(GRP, OPS, None), P(GRP, OPS, None)),
        check_vma=False,
    )
```

time: 183 us -> 217 us (1.19)
  waiting for transfers between devices: 38.5 us -> 65.9 us
  starting transfers between devices: 28 us -> 38.4 us
  blocking collectives: 91.9 us -> 87.1 us
    ppermute x2 -> x3, waiting for transfers between devices: 34.7 us -> 62.2 us  [the longest x1 45.1 us: step(): theirs = lax.ppermute(mine, 'yl', swap)]
    all_to_all x1, starting transfers between devices: 8.98 us -> 17.8 us  [step(): lax.all_to_all(copies, spread, split_axis=0, concat_axis=0, tiled=True)]
    unnamed x1, blocking collectives: 56.6 us -> 49.5 us
    all_gather x1, blocking collectives: 35.3 us -> 37.6 us  [step(): lax.all_gather(jnp.concatenate([mine, theirs], axis=0), 'zh', axis=0, til...]
    ppermute x2 -> x3, starting transfers between devices: 5.57 us -> 7.74 us  [the longest x1 3.26 us: step(): taken = lax.ppermute(given, 'yl', swap)]
  transfers between devices with their start and end apart: 5 -> 6, of which waited for: 2 -> 3; matrix products, arithmetic and copies ran while one was open for 2% -> 2% of each run, Pallas kernels for 0% -> 0%
where the time goes in v3:
time: 217 us; the launch traced here: 216 us
  blocking collectives  87.1 us (40%)
  waiting for transfers between devices  65.9 us (30%)
  starting transfers between devices  38.4 us (18%)
  Pallas kernels  15.3 us (7%)
  local copies, waits for them, and re-layouts  4.36 us (2%)
  between operations  2.84 us (1%)
    unnamed x1, blocking collectives  49.5 us
    ppermute x1, waiting for transfers between devices, step(): theirs = lax.ppermute(mine, 'yl', swap)  45.1 us
    all_gather x1, blocking collectives, step(): lax.all_gather(jnp.concatenate([mine, theirs], axis=0), 'zh', axis=0, til...  37.6 us
    all_to_all x1, starting transfers between devices, step(): lax.all_to_all(copies, spread, split_axis=0, concat_axis=0, tiled=True)  17.8 us
    ppermute x1, waiting for transfers between devices, step(): other = lax.ppermute(own, 'zl', swap)  17.1 us
    all_to_all x1, starting transfers between devices, step(): lax.all_to_all(outgoing, GRP, split_axis=0, concat_axis=0, tiled=True)  11.3 us
    pallas_call x1, Pallas kernels, partial_sums(): pl.pallas_call(kernel, grid_spec=pltpu.PrefetchScalarGridSpec(num_scalar_...  10.7 us
    pallas_call x1, Pallas kernels, outgoing_blocks(): pl.pallas_call(pick_kernel, in_specs=[scalars, scalars, scalars, pl.Block...  4.54 us
  transfers between devices with their start and end apart: 6, of which 3 were waited for; matrix products, arithmetic and copies ran while one was open for 2% of the time, Pallas kernels for 0%

profile of v3, /device:TPU:1, one launch (start us, length us, event | category | flops | bytes accessed | tf_op | source)
XLA Modules:
  0.0 216.0 jit_solution(15167965881718841560)
XLA Ops:
  0.6 4.5 %pick.1 = bf16[16,384,384]{2,1,0:T(8,128)(2,1)} custom-call(s32[112]{0:T(128)} %bitcast.27, s32[112]{0:T(128)} %slots_ref.1, s32[1]{0:T(128)} %bitcast.1.me_ref.refs_1_, bf16[7,384,384]{2,1,0:T(8,128)(2,1)} %bitcast.22), custom_call_target="tpu_custom_call" | custom-call | tf_op jit(solution)/shard_map/pick/pallas_call | solution.py:38
  5.2 11.3 %all-to-all-start = ((bf16[16,384,384]{2,1,0:T(8,128)(2,1)}), bf16[16,384,384]{2,1,0:T(8,128)(2,1)}, u32[]{:S(2)}, u32[]{:S(2)}) async-start(bf16[16,384,384]{2,1,0:T(8,128)(2,1)} %pick.1), calls=%async_computation | async-start | bytes 9437184 | tf_op jit(solution)/shard_map/all_to_all | solution.py:151
  16.5 1.9 collective-permute-start
  18.4 45.1 %collective-permute-done = bf16[12,7,384]{2,0,1:T(8,128)(2,1)S(1)} collective-permute-done((bf16[12,7,384]{2,0,1:T(8,128)(2,1)S(1)}, bf16[12,7,384]{2,0,1:T(8,128)(2,1)S(1)}, u32[]{:S(2)}, u32[]{:S(2)}) %collective-permute-start) | collective-permute-done | bytes 64544 | tf_op jit(solution)/shard_map/ppermute | solution.py:149
  63.6 37.6 %all_gather.3 = bf16[192,7,384]{2,0,1:T(8,128)(2,1)S(1)} all-gather(bf16[24,7,384]{2,0,1:T(8,128)(2,1)S(1)} %pad_maximum_fusion), channel_id=1, replica_groups=mesh['yh'=2,'x'=4,'c'=2,'yl'=2,'zh'=8,'zl'=2] {'zh'}, dimensions={0}, use_global_device_ids=true | all-gather | bytes 1161216 | tf_op jit(solution)/shard_map/all_gather | solution.py:152
  101.2 2.6 %collective-permute-start.1 = (bf16[7,192,384]{2,1,0:T(8,128)(2,1)S(1)}, bf16[7,192,384]{2,1,0:T(8,128)(2,1)S(1)}, u32[]{:S(2)}, u32[]{:S(2)}) collective-permute-start(bf16[7,192,384]{2,1,0:T(8,128)(2,1)S(1)} %bitcast.20), channel_id=1, source_target_pairs={{0,1},{1,0},{2,3},{3,2},{4,5},{5,4},{6,7},{7,6},{8,9},{9,8},{10,11... | collective-permute-start | bytes 3096584 | tf_op jit(solution)/shard_map/ppermute | solution.py:154
  103.7 0.6 pad_add_fusion.refs_2_
  104.4 0.5 bitcast_reduce_fusion
  104.9 17.1 %collective-permute-done.1.refs_5_ = bf16[7,192,384]{2,1,0:T(8,128)(2,1)S(1)} collective-permute-done((bf16[7,192,384]{2,1,0:T(8,128)(2,1)S(1)}, bf16[7,192,384]{2,1,0:T(8,128)(2,1)S(1)}, u32[]{:S(2)}, u32[]{:S(2)}) %collective-permute-start.1) | collective-permute-done | bytes 1032224 | tf_op jit(solution)/shard_map/ppermute | solution.py:154
  122.0 1.0 copy-done.1
  123.0 10.7 %partial.1 = f32[8128,128]{1,0:T(8,128)} custom-call(s32[112]{0:T(128)} %bitcast.28, s32[1]{0:T(128)} %bitcast.1.me_ref.refs_1_, s32[2]{0:T(128)} %pad_add_fusion.refs_2_, f32[1,128]{1,0:T(1,128)} %bitcast.29, bf16[7,192,384]{2,1,0:T(8,128)(2,1)} %bitcast.21, bf16[7,192,384]{2,1,0:T(8,128)(2,1)} %copy-done.1, bf16[7,384,384]{2,1,0:T(8,128)(2,1)} %bitcast.23, ...), custom_call_target="tpu_custom_call" | custom-call | tf_op jit(solution)/shard_map/partial/pallas_call | solution.py:112
  133.7 49.5 %fusion = f32[512,128]{1,0:T(8,128)S(1)} fusion(f32[8128,128]{1,0:T(8,128)} %partial.1), kind=kCustom, calls=%all-reduce-scatter | all-reduce-scatter fusion | flops 1048577 | bytes 4425728
  183.2 1.6 collective-permute-start.3
  184.8 1.3 dynamic-slice.4
  186.7 0.7 concatenate.4
  187.5 0.6 broadcast_in_dim.2
  188.1 17.8 %all-to-all-start.1 = ((f32[32,2,128]{2,1,0:T(2,128)}), f32[32,2,128]{2,1,0:T(2,128)S(1)}, u32[]{:S(2)}, u32[]{:S(2)}) async-start(f32[32,2,128]{2,1,0:T(2,128)} %broadcast_in_dim.2), calls=%async_computation.1 | async-start | bytes 65536 | tf_op jit(solution)/shard_map/all_to_all | solution.py:173
  205.9 3.3 %collective-permute-start.2 = (f32[252,128]{1,0:T(8,128)S(1)}, f32[252,128]{1,0:T(8,128)S(1)}, u32[]{:S(2)}, u32[]{:S(2)}) collective-permute-start(f32[252,128]{1,0:T(8,128)S(1)} %constant_dynamic-slice_fusion.1), channel_id=1, source_target_pairs={{0,16},{16,0},{1,17},{17,1},{2,18},{18,2},{3,19},{19,3},{4,20},{20... | collective-permute-start | bytes 387080 | tf_op jit(solution)/shard_map/ppermute | solution.py:169
  209.2 3.8 %all-to-all-done.1 = f32[32,2,128]{2,1,0:T(2,128)S(1)} async-done(((f32[32,2,128]{2,1,0:T(2,128)}), f32[32,2,128]{2,1,0:T(2,128)S(1)}, u32[]{:S(2)}, u32[]{:S(2)}) %all-to-all-start.1) | async-done | bytes 32800 | tf_op jit(solution)/shard_map/all_to_all | solution.py:173
  212.9 0.1 reduce_sum.32
  213.1 0.6 fusion.5
  215.1 0.1 copy.17
  215.2 0.1 reshape.27
  215.3 0.7 fusion.4
  (21 shorter events, 0.2 us)
Async XLA Ops:
  5.2 11.3 %copy-start.2 = (bf16[7,12,384]{2,0,1:T(8,128)(2,1)S(1)}, bf16[7,12,384]{2,0,1:T(8,128)(2,1)}, u32[]{:S(2)}) copy-start(bf16[7,12,384]{2,0,1:T(8,128)(2,1)} %param.6) | copy-start | bytes 193540
  5.2 116.8 %all-to-all-start = ((bf16[16,384,384]{2,1,0:T(8,128)(2,1)}), bf16[16,384,384]{2,1,0:T(8,128)(2,1)}, u32[]{:S(2)}, u32[]{:S(2)}) async-start(bf16[16,384,384]{2,1,0:T(8,128)(2,1)} %pick.1), calls=%async_computation | async-start | bytes 9437184 | tf_op jit(solution)/shard_map/all_to_all | solution.py:151
  16.5 47.0 %collective-permute-start = (bf16[12,7,384]{2,0,1:T(8,128)(2,1)S(1)}, bf16[12,7,384]{2,0,1:T(8,128)(2,1)S(1)}, u32[]{:S(2)}, u32[]{:S(2)}) collective-permute-start(bf16[12,7,384]{2,0,1:T(8,128)(2,1)S(1)} %bitcast.25), channel_id=1, source_target_pairs={{0,16},{16,0},{1,17},{17,1},{2,18},{18,2},{3,19},{19,3},{4,20},{20... | collective-permute-start | bytes 193544 | tf_op jit(solution)/shard_map/ppermute | solution.py:149
  101.2 20.8 %copy-start = (bf16[192,7,384]{2,0,1:T(8,128)(2,1)}, bf16[192,7,384]{2,0,1:T(8,128)(2,1)S(1)}, u32[]{:S(2)}) copy-start(bf16[192,7,384]{2,0,1:T(8,128)(2,1)S(1)} %all_gather.3) | copy-start | bytes 3096580
  101.2 20.8 %collective-permute-start.1 = (bf16[7,192,384]{2,1,0:T(8,128)(2,1)S(1)}, bf16[7,192,384]{2,1,0:T(8,128)(2,1)S(1)}, u32[]{:S(2)}, u32[]{:S(2)}) collective-permute-start(bf16[7,192,384]{2,1,0:T(8,128)(2,1)S(1)} %bitcast.20), channel_id=1, source_target_pairs={{0,1},{1,0},{2,3},{3,2},{4,5},{5,4},{6,7},{7,6},{8,9},{9,8},{10,11... | collective-permute-start | bytes 3096584 | tf_op jit(solution)/shard_map/ppermute | solution.py:154
  122.0 1.0 copy-start.1
  133.7 81.6 %copy-start.4 = (f32[7,12,384]{2,0,1:T(8,128)S(1)}, f32[7,12,384]{2,0,1:T(8,128)}, u32[]{:S(2)}) copy-start(f32[7,12,384]{2,0,1:T(8,128)} %param.11) | copy-start | bytes 387076
  183.2 3.5 %collective-permute-start.3 = (f32[60,128]{1,0:T(8,128)S(1)}, f32[60,128]{1,0:T(8,128)S(1)}, u32[]{:S(2)}, u32[]{:S(2)}) collective-permute-start(f32[60,128]{1,0:T(8,128)S(1)} %slice.13), channel_id=1, source_target_pairs={{0,1},{1,2},{2,3},{3,4},{4,5},{5,6},{6,7},{7,8},{8,9},{9,10},{10,1... | collective-permute-start | bytes 92168
  188.1 24.8 %all-to-all-start.1 = ((f32[32,2,128]{2,1,0:T(2,128)}), f32[32,2,128]{2,1,0:T(2,128)S(1)}, u32[]{:S(2)}, u32[]{:S(2)}) async-start(f32[32,2,128]{2,1,0:T(2,128)} %broadcast_in_dim.2), calls=%async_computation.1 | async-start | bytes 65536 | tf_op jit(solution)/shard_map/all_to_all | solution.py:173
  205.9 9.1 %collective-permute-start.2 = (f32[252,128]{1,0:T(8,128)S(1)}, f32[252,128]{1,0:T(8,128)S(1)}, u32[]{:S(2)}, u32[]{:S(2)}) collective-permute-start(f32[252,128]{1,0:T(8,128)S(1)} %constant_dynamic-slice_fusion.1), channel_id=1, source_target_pairs={{0,16},{16,0},{1,17},{17,1},{2,18},{18,2},{3,19},{19,3},{4,20},{20... | collective-permute-start | bytes 387080 | tf_op jit(solution)/shard_map/ppermute | solution.py:169
  215.2 0.7 copy-start.3
